TPU v7x, 32 devices: a whole 2x2x4 slice. The times are simulated.
32 devices in a mesh: sec: 16 (over z, y, core), rad: 2 (over x).
Axes of the slice: x: 2, y: 2, z: 4, core: 2. Of those that a mesh axis runs over, the one named last changes fastest.
Arguments:
- transmembrane_potential: float32 [4096, 256], P(('sec', 'rad')), may hold values from -0.8 to -0.3
- channel_openness: float32 [3, 4096, 256], P(None, ('sec', 'rad')), may hold values from 0.02 to 0.95
- longitudinal_conductance: float32 [4096], P(('sec', 'rad')), may hold values from 0.05 to 0.4
- sector_map: int32 [4096, 1], P(('sec', 'rad')), may hold values from 0 to 15; in each aligned block of 128 rows (0 to 127, 128 to 255, ...) at most 16 rows name the same one
- cell_index: int32 [4096], P(('sec', 'rad')), may hold values from 0 to 4095
- innervating_neuron: int32 [4096], P(('sec', 'rad')), may hold values from 0 to 511
- activation_moment: int32 [512], replicated, may hold values from 0 to 19
- synapse_position: int32 [4096], P(('sec', 'rad')), may hold values from 64 to 191
- radial_basis_matrix: float32 [256, 256], replicated, may hold values from -0.375 to 0.375
- spectrum: float32 [256, 512], P('sec'), may hold values from 1 to 20
Outputs:
- transmembrane_potential_later: float32 [4096, 256], P(('sec', 'rad'))
- channel_openness_later: float32 [3, 4096, 256], P(None, ('sec', 'rad'))
- potential: float32 [256, 256, 2, 512], P('sec', 'rad')
Inputs may be any that keep to these rules, and one draw needn't show every extreme that they name: `sector_map`: among the 128 fibres of one device, at most 16 lie in any one sector.
All inputs are finite; a program needn't handle non-finite values.
Results may differ from a plain program's by a relative error of at most 0.00007.
Values sent between devices are 32-bit elements; how exact they have to be, the bound alone decides.
No kernel may reach another device: no remote copies, remote signals or barrier semaphores. Data moves between devices by JAX's collectives and lax.ppermute only.
A program may use at most 64 MiB of HBM per device.

v0:
```python
import math

import jax
import jax.numpy as jnp
from jax import lax
from jax.sharding import PartitionSpec as P

AZ = 512
RAD = 256
SUBSTEPS = 10


TIME_STEP = 0.005
G_SODIUM = 120.0
G_POTASSIUM = 36.0
G_LEAK = 0.3
E_SODIUM = 50.0
E_POTASSIUM = -77.0
E_LEAK = -54.4
APPLIED_AMPERES = 800.0


def second_diff(values):
    left_side = jnp.concatenate([values[:, :1], values[:, :-1]], 1)
    right_side = jnp.concatenate([values[:, 1:], values[:, -1:]], 1)
    return left_side + right_side - 2.0 * values


def sarcolemma_model(
    transmembrane_potential,
    channel_openness,
    longitudinal_conductance,
    activation_substep_count,
    synapse_position,
):
    points = lax.broadcasted_iota(jnp.int32, transmembrane_potential.shape, 1)
    destination_position = (points == synapse_position[:, None]).astype(jnp.float32)

    def substep(present_substep_counter, state_pair):
        volt_now, gate_now = state_pair
        membrane_mv = 100.0 * volt_now
        ionic = (
            G_SODIUM * gate_now[0] ** 3 * gate_now[1] * (membrane_mv - E_SODIUM)
            + G_POTASSIUM * gate_now[2] ** 4 * (membrane_mv - E_POTASSIUM)
            + G_LEAK * (membrane_mv - E_LEAK)
        )
        activation_markers = (present_substep_counter >= activation_substep_count)[:, None].astype(
            jnp.float32
        )
        applied_excitation = APPLIED_AMPERES * destination_position * activation_markers
        opening = jnp.stack(
            [
                jax.nn.softplus((membrane_mv + 40.0) / 10.0),
                0.07 * jnp.exp(-(membrane_mv + 65.0) / 20.0),
                0.1 * jax.nn.softplus((membrane_mv + 55.0) / 10.0),
            ]
        )
        closing = jnp.stack(
            [
                4.0 * jnp.exp(-(membrane_mv + 65.0) / 18.0),
                jax.nn.sigmoid((membrane_mv + 35.0) / 10.0),
                0.125 * jnp.exp(-(membrane_mv + 65.0) / 80.0),
            ]
        )
        rate_sum = opening + closing
        steady = opening / rate_sum
        gate_after = steady + (gate_now - steady) * jnp.exp(-TIME_STEP * rate_sum)
        volt_after = (
            volt_now
            + longitudinal_conductance[:, None] * second_diff(volt_now)
            + TIME_STEP / 100.0 * (applied_excitation - ionic)
        )
        return (volt_after, gate_after)

    return lax.fori_loop(0, SUBSTEPS, substep, (transmembrane_potential, channel_openness))


def per_device(
    transmembrane_potential,
    channel_openness,
    longitudinal_conductance,
    sector_map,
    cell_index,
    innervating_neuron,
    activation_moment,
    synapse_position,
    radial_basis_matrix,
    spectrum,
):
    fibres, point_count = transmembrane_potential.shape
    unit_count = activation_moment.shape[0]
    unit_ids = lax.broadcasted_iota(jnp.int32, (fibres, unit_count), 1)
    activation_substep_count = jnp.sum(
        jnp.where(innervating_neuron[:, None] == unit_ids, activation_moment[None, :], 0), 1
    )
    transmembrane_potential_later, channel_openness_later = sarcolemma_model(
        transmembrane_potential,
        channel_openness,
        longitudinal_conductance,
        activation_substep_count,
        synapse_position,
    )
    source = longitudinal_conductance[:, None] * second_diff(transmembrane_potential_later)
    sectors = lax.axis_size("sec")
    band_count = lax.axis_size("rad")
    sector_width = AZ // sectors
    band_rows = RAD // band_count
    cell_count = sector_width * band_rows
    capacity = 2 * fibres // sectors
    slot_count = sectors * capacity
    chosen = sector_map[:, 0]
    member = (chosen[:, None] == lax.broadcasted_iota(jnp.int32, (fibres, sectors), 1)).astype(
        jnp.int32
    )
    slot_rank = jnp.sum(member * (jnp.cumsum(member, 0) - 1), 1)
    destination = chosen * capacity + slot_rank
    slot_ids = lax.broadcasted_iota(jnp.int32, (slot_count, fibres), 0)
    deposit_placement = (slot_ids == destination[None, :]).astype(jnp.float32)
    placed = jnp.dot(
        deposit_placement,
        source,
        precision=lax.Precision.HIGHEST,
        preferred_element_type=jnp.float32,
    )
    cell_code = cell_index % band_rows * sector_width + cell_index // band_rows + 1
    slot_codes = jnp.dot(
        deposit_placement,
        cell_code.astype(jnp.float32),
        precision=lax.Precision.HIGHEST,
        preferred_element_type=jnp.float32,
    )
    slab_width = point_count // band_count
    pieces = placed.reshape(slot_count, band_count, slab_width)
    spread_codes = jnp.broadcast_to(slot_codes[:, None], (slot_count, band_count))
    pieces, spread_codes = (
        lax.all_to_all(
            lax.all_to_all(pieces, "sec", split_axis=0, concat_axis=0, tiled=True),
            "rad",
            split_axis=1,
            concat_axis=1,
            tiled=True,
        ),
        lax.all_to_all(
            lax.all_to_all(spread_codes, "sec", split_axis=0, concat_axis=0, tiled=True),
            "rad",
            split_axis=1,
            concat_axis=1,
            tiled=True,
        ),
    )
    cell_ids = lax.broadcasted_iota(jnp.int32, (slot_count, band_count, cell_count), 2)
    onehot = (spread_codes.astype(jnp.int32)[:, :, None] - 1 == cell_ids).astype(jnp.float32)
    deposited = jnp.einsum("snx,snc->xnc", pieces, onehot, precision=lax.Precision.HIGHEST)
    radial_field = deposited.reshape(slab_width, RAD, sector_width)
    projected = jnp.einsum(
        "xra,rj->jxa", radial_field, radial_basis_matrix, precision=lax.Precision.HIGHEST
    )
    all_azimuths = lax.all_to_all(projected, "sec", split_axis=0, concat_axis=2, tiled=True)
    basis_local = all_azimuths.shape[0]
    slab_local = all_azimuths.shape[1]
    row_ids = lax.broadcasted_iota(jnp.int32, (AZ, AZ), 0)
    col_ids = lax.broadcasted_iota(jnp.int32, (AZ, AZ), 1)
    phase = (row_ids * col_ids % AZ).astype(jnp.float32) * (2.0 * math.pi / AZ)
    dft_table = jnp.concatenate([jnp.cos(phase), -jnp.sin(phase)], 1) * (1.0 / math.sqrt(AZ))
    flattened = all_azimuths.reshape(basis_local * slab_local, AZ)
    spectral = jnp.dot(
        flattened, dft_table, precision=lax.Precision.HIGHEST, preferred_element_type=jnp.float32
    )
    spectral = spectral.reshape(basis_local, slab_local, 2, AZ)
    potential = spectral * spectrum[:, None, None, :]
    return (transmembrane_potential_later, channel_openness_later, potential)


def solution(mesh):
    placed = (
        P(("sec", "rad"), None),
        P(None, ("sec", "rad"), None),
        P(("sec", "rad")),
        P(("sec", "rad"), None),
        P(("sec", "rad")),
        P(("sec", "rad")),
        P(),
        P(("sec", "rad")),
        P(),
        P("sec", None),
    )
    return jax.shard_map(
        per_device,
        mesh=mesh,
        in_specs=placed,
        out_specs=(
            P(("sec", "rad"), None),
            P(None, ("sec", "rad"), None),
            P("sec", "rad", None, None),
        ),
        check_vma=False,
    )
```

profile of v0, /device:TPU:13, one launch (start us, length us, event | category | flops | bytes accessed | tf_op | source)
XLA Modules:
  0.0 218.9 jit_solution(2424597692207753991)
XLA Ops:
  0.6 0.9 copy.69
  1.6 1.0 copy.70
  2.6 0.7 fusion.46
  3.3 0.2 reduce_window_sum.11
  3.5 0.8 select_reduce_fusion.1
  4.3 0.7 multiply_add_fusion.2
  5.0 0.8 fusion.41
  5.8 0.1 broadcast_in_dim.35
  5.9 0.7 broadcast_in_dim.36
  6.5 6.5 %all-to-all-start = ((f32[16,16,2]{1,2,0:T(2,128)}), f32[16,16,2]{1,2,0:T(2,128)S(1)}, u32[]{:S(2)}, u32[]{:S(2)}) async-start(f32[16,16,2]{1,2,0:T(2,128)} %broadcast_in_dim.36), calls=%async_computation | async-start | bytes 32768 | tf_op jit(solution)/shard_map/all_to_all | solution.py:144
  13.1 0.9 select_reduce_fusion
  13.9 16.2 %while.18 = (s32[]{:T(128)}, f32[128,256]{1,0:T(8,128)S(1)}, f32[3,128,256]{2,1,0:T(8,128)S(1)}, f32[128]{0:T(128)}, s32[128]{0:T(128)S(1)}, /*index=5*/s32[128]{0:T(128)}, s32[]{:T(128)}) while((s32[]{:T(128)}, f32[128,256]{1,0:T(8,128)S(1)}, f32[3,128,256]{2,1,0:T(8,128)S(1)}, f32[128]{0:T(128)}, s32[128]{0:T(128)S(1)}, ...), condition=%wide.region_2.3_spmd.clone, body=%wide.region_1.2_spmd.clone.sunk | while | flops 2883842 | bytes 3803737 | solution.py:75
  14.0 0.1 fusion.81
  14.1 1.1 fusion.82
  15.2 0.3 multiply_add_fusion.4
  15.6 0.1 fusion.81
  15.8 1.1 fusion.82
  16.8 0.3 multiply_add_fusion.4
  17.3 0.1 fusion.81
  17.4 1.1 fusion.82
  18.5 0.3 multiply_add_fusion.4
  18.8 0.1 fusion.80
  18.9 0.1 fusion.81
  19.0 1.1 fusion.82
  20.1 0.3 multiply_add_fusion.4
  20.5 0.1 fusion.81
  20.6 1.1 fusion.82
  21.7 0.3 multiply_add_fusion.4
  22.1 0.1 fusion.81
  22.2 1.1 fusion.82
  23.3 0.3 multiply_add_fusion.4
  23.8 0.1 fusion.81
  23.9 1.1 fusion.82
  25.0 0.3 multiply_add_fusion.4
  25.4 0.1 fusion.81
  25.5 1.1 fusion.82
  26.6 0.3 multiply_add_fusion.4
  27.0 0.1 fusion.81
  27.1 1.1 fusion.82
  28.2 0.3 multiply_add_fusion.4
  28.6 0.1 fusion.81
  28.7 1.1 fusion.82
  29.8 0.3 multiply_add_fusion.4
  30.3 0.1 fusion.72
  30.4 1.1 fusion.33
  31.5 0.8 copy.41
  32.3 6.0 %all-to-all-start.2 = ((f32[256,2,128]{2,1,0:T(2,128)}), f32[256,2,128]{2,1,0:T(2,128)S(1)}, u32[]{:S(2)}, u32[]{:S(2)}) async-start(f32[256,2,128]{2,1,0:T(2,128)} %copy.41), calls=%async_computation.2 | async-start | bytes 524288 | tf_op jit(solution)/shard_map/all_to_all | solution.py:137
  38.3 0.6 all_to_all.35
  39.0 7.3 %all-to-all-done.2 = f32[256,2,128]{2,1,0:T(2,128)S(1)} async-done(((f32[256,2,128]{2,1,0:T(2,128)}), f32[256,2,128]{2,1,0:T(2,128)S(1)}, u32[]{:S(2)}, u32[]{:S(2)}) %all-to-all-start.2) | async-done | bytes 262176 | tf_op jit(solution)/shard_map/all_to_all | solution.py:137
  46.3 3.2 %all-to-all-start.1 = ((f32[256,2,1]{0,2,1:T(1,128)}), f32[256,2,1]{0,2,1:T(1,128)S(1)}, u32[]{:S(2)}, u32[]{:S(2)}) async-start(f32[256,2,1]{0,2,1:T(1,128)} %all_to_all.35), calls=%async_computation.1 | async-start | bytes 4096 | tf_op jit(solution)/shard_map/all_to_all | solution.py:143
  49.4 0.7 copy.42
  50.1 1.7 all-to-all-done.1
  51.9 3.6 %all-to-all-start.3 = ((f32[256,2,128]{2,0,1:T(8,128)}), f32[256,2,128]{2,0,1:T(8,128)S(1)}, u32[]{:S(2)}, u32[]{:S(2)}) async-start(f32[256,2,128]{2,0,1:T(8,128)} %copy.42), calls=%async_computation.3 | async-start | bytes 524288 | tf_op jit(solution)/shard_map/all_to_all | solution.py:136
  55.5 3.8 %all-to-all-done.3 = f32[256,2,128]{2,0,1:T(8,128)S(1)} async-done(((f32[256,2,128]{2,0,1:T(8,128)}), f32[256,2,128]{2,0,1:T(8,128)S(1)}, u32[]{:S(2)}, u32[]{:S(2)}) %all-to-all-start.3) | async-done | bytes 262176 | tf_op jit(solution)/shard_map/all_to_all | solution.py:136
  59.4 3.8 %fusion.16 = f32[2,4096,128]{2,1,0:T(8,128)S(1)} fusion(f32[256,2,128]{2,0,1:T(8,128)S(1)} %all-to-all-done.3, s32[256,2]{0,1:T(2,128)S(1)} %bitcast.62), kind=kOutput, calls=%fused_computation.32 | convolution fusion | flops 3223322624 | bytes 4458496 | tf_op jit(solution)/shard_map/snx,snc->xnc/dot_general | solution.py:153
  63.2 11.6 %fusion.20 = f32[256,128,32]{0,1,2:T(8,128)} fusion(f32[128,256,32]{0,2,1:T(8,128)S(1)} %bitcast.59, f32[256,256]{1,0:T(8,128)S(1)} %copy-done), kind=kOutput, calls=%fused_computation.37 | convolution fusion | flops 3221225472 | bytes 8650752 | tf_op jit(solution)/shard_map/xra,rj->jxa/dot_general | solution.py:155
  74.8 5.5 %copy.44 = f32[256,128,32]{1,2,0:T(8,128)} copy(f32[256,128,32]{0,1,2:T(8,128)} %fusion.20) | data formatting | bytes 8388608 | tf_op jit(solution)/shard_map/xra,rj->jxa/dot_general | solution.py:155
  80.3 8.9 %all-to-all-start.4 = ((f32[256,128,32]{1,2,0:T(8,128)}), f32[256,128,32]{1,2,0:T(8,128)}, u32[]{:S(2)}, u32[]{:S(2)}) async-start(f32[256,128,32]{1,2,0:T(8,128)} %copy.44), calls=%async_computation.4 | async-start | bytes 8388608 | tf_op jit(solution)/shard_map/all_to_all | solution.py:158
  89.2 4.1 %sine_negate_fusion = (f32[512,512]{0,1:T(8,128)S(1)}, f32[512,512]{0,1:T(8,128)S(1)}) fusion(), kind=kLoop, calls=%fused_computation.45 | loop fusion | flops 3932160 | bytes 2097152 | tf_op jit(solution)/shard_map/neg | solution.py:164
  93.3 0.2 maximum_multiply_fusion
  93.6 88.1 %all-to-all-done.4 = f32[256,128,32]{1,2,0:T(8,128)} async-done(((f32[256,128,32]{1,2,0:T(8,128)}), f32[256,128,32]{1,2,0:T(8,128)}, u32[]{:S(2)}, u32[]{:S(2)}) %all-to-all-start.4) | async-done | bytes 4194336 | tf_op jit(solution)/shard_map/all_to_all | solution.py:158
  181.7 2.8 %copy.45 = f32[16,128,16,32]{1,3,2,0:T(8,128)S(1)} copy(f32[16,128,16,32]{1,3,0,2:T(8,128)} %bitcast.9) | data formatting | bytes 8388608 | tf_op jit(solution)/shard_map/all_to_all | solution.py:158
  184.5 26.4 %broadcast_multiply_fusion = f32[16,128,2,512]{3,1,2,0:T(8,128)S(1)} fusion(f32[16,512]{1,0:T(8,128)S(1)} %copy-done.3, f32[16,128,512,1]{1,2,3,0:T(8,128)S(1)} %bitcast.58, f32[2,512,512,1]{2,1,0,3:T(8,128)S(1)} %bitcast.60), kind=kOutput, calls=%fused_computation.35 | convolution fusion | flops 12886999040 | bytes 14712832 | tf_op jit(solution)/shard_map/dot_general | solution.py:166
  210.9 8.0 %copy.47 = f32[16,128,2,512]{3,2,1,0:T(2,128)} copy(f32[16,128,2,512]{3,1,2,0:T(8,128)S(1)} %broadcast_multiply_fusion) | data formatting | bytes 16777216
  (32 shorter events, 0.9 us)
Async XLA Ops:
  0.6 62.6 %copy-start = (f32[256,256]{1,0:T(8,128)S(1)}, f32[256,256]{1,0:T(8,128)}, u32[]{:S(2)}) copy-start(f32[256,256]{1,0:T(8,128)} %param.20) | copy-start | bytes 786436
  6.5 25.8 %all-to-all-start = ((f32[16,16,2]{1,2,0:T(2,128)}), f32[16,16,2]{1,2,0:T(2,128)S(1)}, u32[]{:S(2)}, u32[]{:S(2)}) async-start(f32[16,16,2]{1,2,0:T(2,128)} %broadcast_in_dim.36), calls=%async_computation | async-start | bytes 32768 | tf_op jit(solution)/shard_map/all_to_all | solution.py:144
  30.2 44.6 %copy-start.1 = (f32[128,256]{1,0:T(8,128)}, f32[128,256]{1,0:T(8,128)S(1)}, u32[]{:S(2)}) copy-start(f32[128,256]{1,0:T(8,128)S(1)} %get-tuple-element.189) | copy-start | bytes 393220
  30.2 44.6 %copy-start.2 = (f32[3,128,256]{2,1,0:T(8,128)}, f32[3,128,256]{2,1,0:T(8,128)S(1)}, u32[]{:S(2)}) copy-start(f32[3,128,256]{2,1,0:T(8,128)S(1)} %get-tuple-element.190) | copy-start | bytes 1179652
  32.3 14.0 %all-to-all-start.2 = ((f32[256,2,128]{2,1,0:T(2,128)}), f32[256,2,128]{2,1,0:T(2,128)S(1)}, u32[]{:S(2)}, u32[]{:S(2)}) async-start(f32[256,2,128]{2,1,0:T(2,128)} %copy.41), calls=%async_computation.2 | async-start | bytes 524288 | tf_op jit(solution)/shard_map/all_to_all | solution.py:137
  46.3 5.6 %all-to-all-start.1 = ((f32[256,2,1]{0,2,1:T(1,128)}), f32[256,2,1]{0,2,1:T(1,128)S(1)}, u32[]{:S(2)}, u32[]{:S(2)}) async-start(f32[256,2,1]{0,2,1:T(1,128)} %all_to_all.35), calls=%async_computation.1 | async-start | bytes 4096 | tf_op jit(solution)/shard_map/all_to_all | solution.py:143
  51.9 7.5 %all-to-all-start.3 = ((f32[256,2,128]{2,0,1:T(8,128)}), f32[256,2,128]{2,0,1:T(8,128)S(1)}, u32[]{:S(2)}, u32[]{:S(2)}) async-start(f32[256,2,128]{2,0,1:T(8,128)} %copy.42), calls=%async_computation.3 | async-start | bytes 524288 | tf_op jit(solution)/shard_map/all_to_all | solution.py:136
  80.3 101.4 %all-to-all-start.4 = ((f32[256,128,32]{1,2,0:T(8,128)}), f32[256,128,32]{1,2,0:T(8,128)}, u32[]{:S(2)}, u32[]{:S(2)}) async-start(f32[256,128,32]{1,2,0:T(8,128)} %copy.44), calls=%async_computation.4 | async-start | bytes 8388608 | tf_op jit(solution)/shard_map/all_to_all | solution.py:158
  181.7 2.8 %copy-start.3 = (f32[16,512]{1,0:T(8,128)S(1)}, f32[16,512]{1,0:T(8,128)}, u32[]{:S(2)}) copy-start(f32[16,512]{1,0:T(8,128)} %param.21) | copy-start | bytes 98308
where the time goes:
time: 220 us; the launch traced here: 219 us
  waiting for transfers between devices  101 us (46%)
  matrix products  43.6 us (20%)
  starting transfers between devices  28.2 us (13%)
  local copies, waits for them, and re-layouts  23.2 us (11%)
  other arithmetic  21.7 us (10%)
    all_to_all x1, waiting for transfers between devices, per_device(): lax.all_to_all(projected, 'sec', split_axis=0, concat_axis=2, tiled=True)  88.1 us
    dot_general x1, matrix products, per_device(): jnp.dot(flattened, dft_table, precision=lax.Precision.HIGHEST, preferred_...  26.4 us
    dot_general x1, matrix products, per_device(): jnp.einsum('xra,rj->jxa', radial_field, radial_basis_matrix, precision=la...  11.6 us
    another operation x10, other arithmetic, substep(): jnp.stack([jax.nn.softplus((membrane_mv + 40.0) / 10.0), 0.07 * jnp.exp(-...  10.9 us
    unnamed x12, local copies, waits for them, and re-layouts  9.93 us
    all_to_all x1, starting transfers between devices, per_device(): lax.all_to_all(projected, 'sec', split_axis=0, concat_axis=2, tiled=True)  8.92 us
    all_to_all x1, waiting for transfers between devices, per_device(): lax.all_to_all(pieces, 'sec', split_axis=0, concat_axis=0, tiled=True)  7.3 us
    all_to_all x1, starting transfers between devices, per_device(): lax.all_to_all(spread_codes, 'sec', split_axis=0, concat_axis=0, tiled=True)  6.52 us
  transfers between devices with their start and end apart: 5, of which 4 were waited for; matrix products, arithmetic and copies ran while one was open for 11% of the time, Pallas kernels for 0%

commit v1 on v0

--- a/solution.py
+++ b/solution.py
@@ -1,8 +1,13 @@
 import math
+
+import functools
 
 import jax
 import jax.numpy as jnp
+import numpy as np
 from jax import lax
+from jax.experimental import pallas as pl
+from jax.experimental.pallas import tpu as pltpu
 from jax.sharding import PartitionSpec as P
 
 AZ = 512
@@ -75,7 +80,7 @@
     return lax.fori_loop(0, SUBSTEPS, substep, (transmembrane_potential, channel_openness))
 
 
-def per_device(
+def per_device_general(
     transmembrane_potential,
     channel_openness,
     longitudinal_conductance,
@@ -171,6 +176,325 @@
     return (transmembrane_potential_later, channel_openness_later, potential)
 
 
+F32 = jnp.float32
+BF16 = jnp.bfloat16
+
+
+def iota(shape, axis):
+    return lax.broadcasted_iota(jnp.int32, shape, axis).astype(F32)
+
+
+def column(row, lanes):
+    count = row.shape[1]
+    wide = jnp.transpose(jnp.broadcast_to(row, (count, count)))
+    return jnp.concatenate([wide] * (lanes // count), 1) if lanes > count else wide
+
+
+def split(values):
+    high = values.astype(BF16)
+    return high, (values - high.astype(F32)).astype(BF16)
+
+
+def fibre_kernel(
+    band_ref,
+    volt_ref,
+    gate_ref,
+    cond_ref,
+    sector_ref,
+    cell_ref,
+    unit_ref,
+    moment_ref,
+    synapse_ref,
+    volt_out,
+    gate_out,
+    pieces_out,
+    fire_scratch,
+    cond_scratch,
+    *,
+    sectors,
+    sector_width,
+    band_rows,
+    chunk,
+):
+    fibres, points = volt_ref.shape
+    bands, _, slab = pieces_out.shape
+    units = moment_ref.shape[1]
+    band = band_ref[0]
+    chosen = (iota((units, fibres), 0) == unit_ref[...].astype(F32)).astype(BF16)
+    moments = jnp.broadcast_to(moment_ref[...].astype(F32), (8, units)).astype(BF16)
+    fire_row = jnp.dot(moments, chosen, preferred_element_type=F32)[:1]
+    at_synapse = iota((fibres, points), 1) == column(synapse_ref[...].astype(F32), points)
+    fire_scratch[...] = jnp.where(at_synapse, column(fire_row, points), 1e6)
+    cond_scratch[...] = column(cond_ref[...], points)
+    volt_out[...] = volt_ref[...]
+    gate_out[...] = gate_ref[...]
+
+    def curvature(values):
+        where = lax.broadcasted_iota(jnp.int32, values.shape, 1)
+        left = jnp.where(where == 0, values, pltpu.roll(values, 1, 1))
+        right = jnp.where(where == points - 1, values, pltpu.roll(values, points - 1, 1))
+        return left + right - 2.0 * values
+
+    def substep(step, carry):
+        now = step.astype(F32)
+        for start in range(0, fibres, chunk):
+            rows = pl.ds(start, chunk)
+            volt = volt_out[rows, :]
+            gate_m, gate_h, gate_n = gate_out[0, rows, :], gate_out[1, rows, :], gate_out[2, rows, :]
+            mv = 100.0 * volt
+            rest = mv + 65.0
+            e80 = jnp.exp(rest * (-1.0 / 80.0))
+            e40 = e80 * e80
+            e20 = e40 * e40
+            e10 = e20 * e20
+            up = jnp.exp(rest * 0.1)
+            alpha_m = jnp.log(1.0 + math.exp(-2.5) * up)
+            alpha_h = 0.07 * e20
+            alpha_n = 0.1 * jnp.log(1.0 + math.exp(-1.0) * up)
+            beta_m = 4.0 * jnp.exp(rest * (-1.0 / 18.0))
+            beta_h = 1.0 / (1.0 + math.exp(3.0) * e10)
+            beta_n = 0.125 * e80
+            square_n = gate_n * gate_n
+            ionic = (
+                G_SODIUM * (gate_m * gate_m * gate_m) * gate_h * (mv - E_SODIUM)
+                + G_POTASSIUM * (square_n * square_n) * (mv - E_POTASSIUM)
+                + G_LEAK * (mv - E_LEAK)
+            )
+            stimulus = jnp.where(now >= fire_scratch[rows, :], APPLIED_AMPERES, 0.0)
+            for index, (gate, alpha, beta) in enumerate(
+                ((gate_m, alpha_m, beta_m), (gate_h, alpha_h, beta_h), (gate_n, alpha_n, beta_n))
+            ):
+                rate = alpha + beta
+                steady = alpha / rate
+                gate_out[index, rows, :] = steady + (gate - steady) * jnp.exp(-TIME_STEP * rate)
+            volt_out[rows, :] = (
+                volt
+                + cond_scratch[rows, :] * curvature(volt)
+                + (TIME_STEP / 100.0) * (stimulus - ionic)
+            )
+        return carry
+
+    lax.fori_loop(0, SUBSTEPS, substep, 0)
+    source = cond_scratch[...] * curvature(volt_out[...])
+
+    sector = sector_ref[...].astype(F32)
+    earlier = (column(sector, fibres) == sector) & (iota((fibres, fibres), 0) < iota((fibres, fibres), 1))
+    rank = jnp.sum(earlier.astype(F32), 0, keepdims=True)
+    capacity = 2 * fibres // sectors
+    slot = sector * capacity + rank
+    cell = cell_ref[...]
+    within = cell // band_rows
+    half = sector_width // 2
+    ordered = (within % 2) * half + within // 2
+    radius = (cell % band_rows).astype(F32) + (band * band_rows).astype(F32)
+    in_sector = (iota((sectors, fibres), 0) == sector).astype(F32)
+    digits = jnp.concatenate(
+        [in_sector * radius, in_sector * (ordered.astype(F32) + 1.0)], 0
+    ).astype(BF16)
+    in_rank = (column(rank, fibres) == iota((fibres, fibres), 1)).astype(BF16)
+    table = jnp.dot(digits, in_rank, preferred_element_type=F32)
+    table = table[:sectors] + (bands * band_rows) * table[sectors:]
+    meta = table[:8]
+    for group in range(1, sectors // 8):
+        meta = meta + pltpu.roll(table[8 * group : 8 * group + 8], group * capacity, 1)
+    slots = jnp.broadcast_to(slot, (8, fibres))
+    lane, line = iota((8, fibres), 1), iota((8, fibres), 0)
+    middle = fibres // 2
+    meta = jnp.where((lane >= middle) & (line == 0), pltpu.roll(slots, middle, 1), meta)
+    meta = jnp.where((lane >= middle) & (line == 1), slots, meta)
+    for offset in range(bands):
+        lanes = pl.ds(pl.multiple_of(((band + offset) % bands) * slab, slab), slab)
+        fire_scratch[...] = source
+        pieces_out[offset, :fibres, :] = fire_scratch[:, lanes]
+        pieces_out[offset, fibres:, :] = meta
+
+
+def grid_kernel(start_ref, *refs, count, sectors, sector_width, group):
+    pieces = refs[:count]
+    basis_ref, table_high, table_low, spectrum_ref, out_ref, placed, columns, basis_t, scales = refs[count:]
+    fibres = pieces[0].shape[0] - 8
+    slab = pieces[0].shape[1]
+    capacity = 2 * fibres // sectors
+    radii = basis_ref.shape[0]
+    own = spectrum_ref.shape[0]
+    slots = sectors * capacity
+    depth = count * capacity
+    half = sector_width // 2
+    step = pl.program_id(0)
+
+    @pl.when(step == 0)
+    def _():
+        basis_t[...] = jnp.transpose(basis_ref[...])
+        for j in range(own):
+            scales[j] = jnp.broadcast_to(spectrum_ref[j : j + 1, :], scales.shape[1:])
+        mine = basis_t[pl.ds(pl.multiple_of(start_ref[0], 8), own), :]
+        basis_pair = jnp.concatenate(split(mine), 0)
+        lane8 = lax.broadcasted_iota(jnp.int32, (8, slab), 1)
+        code_parts = [[jnp.zeros((8, slab), F32) for _ in range(depth // slab)] for _ in range(sectors // 8)]
+        per = slab // capacity
+        for d in range(count):
+            values = pieces[d][:fibres, :]
+            meta = pieces[d][fibres:, :]
+            slot = jnp.where(lane8[:1] < fibres // 2, pltpu.roll(meta[0:1], fibres // 2, 1), meta[1:2])
+            chosen = (iota((slots, fibres), 0) == slot).astype(BF16)
+            both = jnp.concatenate(split(values), 1)
+            sorted_ = jnp.dot(chosen, both, preferred_element_type=F32).astype(BF16)
+            for s in range(sectors):
+                placed[s, d * capacity : (d + 1) * capacity, :] = sorted_[s * capacity : (s + 1) * capacity]
+            at = (d % per) * capacity
+            inside = (lane8 >= at) & (lane8 < at + capacity)
+            for g in range(sectors // 8):
+                moved = pltpu.roll(meta, (at - g * capacity) % slab, 1)
+                code_parts[g][d // per] = jnp.where(inside, moved, code_parts[g][d // per])
+        codes = [jnp.concatenate(parts, 1) for parts in code_parts]
+        for s in range(sectors):
+            code = codes[s // 8][s % 8 : s % 8 + 1]
+            within = jnp.floor(code * (1.0 / radii))
+            radius = code - radii * within
+            at_radius = (iota((radii, depth), 0) == radius).astype(BF16)
+            rows = jnp.dot(basis_pair, at_radius, preferred_element_type=F32).astype(BF16)
+            mask = (iota((sector_width, depth), 0) + 1.0 == within).astype(BF16)
+            weights = (rows[:, None, :] * mask[None]).reshape(2 * own * sector_width, depth)
+            product = jnp.dot(weights, placed[s], preferred_element_type=F32)
+            size = own * sector_width
+            total = product[:size, :slab] + product[:size, slab:] + product[size:, :slab]
+            for j in range(own):
+                for e in range(2):
+                    first = j * sector_width + e * half
+                    columns[j, e, s * half : (s + 1) * half, :] = total[first : first + half]
+
+    parts = []
+    quarter = table_high.shape[2] // 2
+    for e in range(2):
+        turned = [jnp.transpose(columns[step * group + i, e]) for i in range(group)]
+        high, low = split(jnp.concatenate(turned, 0))
+        parts.append(
+            jnp.dot(high, table_high[e], preferred_element_type=F32)
+            + jnp.dot(low, table_high[e], preferred_element_type=F32)
+            + jnp.dot(high, table_low[e], preferred_element_type=F32)
+        )
+    total, difference = parts[0] + parts[1], parts[0] - parts[1]
+    tiles = quarter // 128
+    for i in range(group):
+        for c in range(2):
+            for t in range(2 * tiles):
+                source = total if t < tiles else difference
+                lanes = c * quarter + (t % tiles) * 128
+                scale = scales[step * group + i, :1, t * 128 : (t + 1) * 128]
+                value = source[i * slab : (i + 1) * slab, lanes : lanes + 128] * scale
+                line = (4 * tiles) * slab * i + 2 * t + c
+                out_ref[pl.ds(line, slab, stride=4 * tiles), :] = value
+
+
+def dft_tables():
+    half = AZ // 2
+    wave, place = np.meshgrid(np.arange(half), np.arange(half))
+    tables = []
+    for e in range(2):
+        phase = (wave * (2 * place + e) % AZ) * (2.0 * np.pi / AZ)
+        tables.append(np.concatenate([np.cos(phase), -np.sin(phase)], 1) / np.sqrt(AZ))
+    exact = np.stack(tables).astype(np.float32)
+    high = jnp.asarray(exact).astype(BF16)
+    low = (jnp.asarray(exact) - high.astype(F32)).astype(BF16)
+    return high, low
+
+
+def gather(pieces):
+    sectors = lax.axis_size("sec")
+
+    def swap(value, bits):
+        return lax.ppermute(value, "sec", [(i, i ^ bits) for i in range(sectors)])
+
+    other = lax.ppermute(pieces[1], "rad", [(0, 1), (1, 0)])
+    held = []
+    for value in (pieces[0], other):
+        along = [value] + [swap(value, bits) for bits in range(4, sectors, 4)]
+        across = along + [swap(v, 2) for v in along]
+        held += across + [swap(v, 1) for v in across]
+    return held
+
+
+def per_device(
+    transmembrane_potential,
+    channel_openness,
+    longitudinal_conductance,
+    sector_map,
+    cell_index,
+    innervating_neuron,
+    activation_moment,
+    synapse_position,
+    radial_basis_matrix,
+    spectrum,
+):
+    fibres, points = transmembrane_potential.shape
+    sectors, bands = lax.axis_size("sec"), lax.axis_size("rad")
+    slab = points // bands
+    sector_width = AZ // sectors
+    own = spectrum.shape[0]
+    vmem = pl.BlockSpec(memory_space=pltpu.VMEM)
+    smem = pl.BlockSpec(memory_space=pltpu.SMEM)
+    band = lax.axis_index("rad").astype(jnp.int32).reshape(1)
+    volt, gates, pieces = pl.pallas_call(
+        functools.partial(
+            fibre_kernel,
+            sectors=sectors,
+            sector_width=sector_width,
+            band_rows=RAD // bands,
+            chunk=16,
+        ),
+        out_shape=(
+            jax.ShapeDtypeStruct((fibres, points), F32),
+            jax.ShapeDtypeStruct((3, fibres, points), F32),
+            jax.ShapeDtypeStruct((bands, fibres + 8, slab), F32),
+        ),
+        in_specs=[smem] + [vmem] * 8,
+        out_specs=(vmem, vmem, vmem),
+        scratch_shapes=[pltpu.VMEM((fibres, points), F32), pltpu.VMEM((fibres, points), F32)],
+    )(
+        band,
+        transmembrane_potential,
+        channel_openness,
+        longitudinal_conductance.reshape(1, fibres),
+        sector_map.reshape(1, fibres),
+        cell_index.reshape(1, fibres),
+        innervating_neuron.reshape(1, fibres),
+        activation_moment.reshape(1, -1),
+        synapse_position.reshape(1, fibres),
+    )
+    held = gather(pieces)
+    count = len(held)
+    capacity = 2 * fibres // sectors
+    group = 4
+    high, low = dft_tables()
+    start = (lax.axis_index("sec") * own).astype(jnp.int32).reshape(1)
+    lines = own * slab * 2 * AZ // 128
+
+    def whole(array):
+        rank = len(array.shape)
+        return pl.BlockSpec(array.shape, lambda g: (0,) * rank, pipeline_mode=pl.Buffered(1))
+
+    flat = pl.pallas_call(
+        functools.partial(
+            grid_kernel, count=count, sectors=sectors, sector_width=sector_width, group=group
+        ),
+        out_shape=jax.ShapeDtypeStruct((lines, 128), F32),
+        grid=(own // group,),
+        in_specs=[smem]
+        + [whole(v) for v in held]
+        + [whole(v) for v in (radial_basis_matrix, high, low, spectrum)],
+        out_specs=pl.BlockSpec((lines * group // own, 128), lambda g: (g, 0)),
+        scratch_shapes=[
+            pltpu.VMEM((sectors, count * capacity, 2 * slab), BF16),
+            pltpu.VMEM((own, 2, AZ // 2, slab), F32),
+            pltpu.VMEM((RAD, RAD), F32),
+            pltpu.VMEM((own, 8, AZ), F32),
+        ],
+    )(start, *held, radial_basis_matrix, high, low, spectrum)
+    tiled = flat.reshape(own, slab, AZ // 128, 2, 128)
+    potential = tiled.transpose(0, 1, 3, 2, 4).reshape(own, slab, 2, AZ)
+    return volt, gates, potential
+
+
 def solution(mesh):
     placed = (
         P(("sec", "rad"), None),
@@ -184,8 +508,9 @@
         P(),
         P("sec", None),
     )
+    fits = mesh.shape["rad"] == 2 and mesh.shape["sec"] == 16
     return jax.shard_map(
-        per_device,
+        per_device if fits else per_device_general,
         mesh=mesh,
         in_specs=placed,
         out_specs=(

time: 220 us -> 59.2 us (0.27)
  the two profiles are of different devices: /device:TPU:13 before, /device:TPU:0 now
where the time goes in v1:
time: 59.2 us; the launch traced here: 59 us
  starting transfers between devices  23.6 us (40%)
  Pallas kernels  22 us (37%)
  waiting for transfers between devices  11 us (19%)
  local copies, waits for them, and re-layouts  1.39 us (2%)
  between operations  1.03 us (2%)
    ppermute x30, starting transfers between devices, swap(): return lax.ppermute(value, 'sec', [(i, i ^ bits) for i in range(sectors)])  20.6 us
    pallas_call x1, Pallas kernels, per_device(): pl.pallas_call(functools.partial(grid_kernel, count=count, sectors=sector...  15.8 us
    ppermute x30, waiting for transfers between devices, swap(): return lax.ppermute(value, 'sec', [(i, i ^ bits) for i in range(sectors)])  11 us
    pallas_call x1, Pallas kernels, per_device(): pl.pallas_call(functools.partial(fibre_kernel, sectors=sectors, sector_wi...  6.19 us
    ppermute x1, starting transfers between devices, gather(): other = lax.ppermute(pieces[1], 'rad', [(0, 1), (1, 0)])  3.03 us
  transfers between devices with their start and end apart: 31, of which 10 were waited for; matrix products, arithmetic and copies ran while one was open for 0% of the time, Pallas kernels for 0%

profile of v1, /device:TPU:0, one launch (start us, length us, event | category | flops | bytes accessed | tf_op | source)
XLA Modules:
  0.0 59.0 jit_solution(5255872386710182008)
XLA Ops:
  0.6 6.2 %shard_map.130 = (f32[128,256]{1,0:T(8,128)}, f32[3,128,256]{2,1,0:T(8,128)}, f32[2,136,128]{2,1,0:T(8,128)}) custom-call(s32[1]{0:T(128)} %bitcast.band_ref, f32[128,256]{1,0:T(8,128)} %volt_ref.1, f32[3,128,256]{2,1,0:T(8,128)} %gate_ref.1, f32[1,128]{1,0:T(1,128)} %bitcast.19, s32[1,128]{1,0:T(1,128)} %bitcast.20, s32[1,128]{1,0:T(1,128)} %bitcast.21, ...), custom_call_target="tpu_custom_call" | custom-call | tf_op jit(solution)/shard_map/pallas_call | solution.py:437
  6.8 0.9 %slice_bitcast_fusion = (f32[136,128]{1,0:T(8,128)S(1)}, f32[136,128]{1,0:T(8,128)S(1)}) fusion(f32[2,136,128]{2,1,0:T(8,128)} %get-tuple-element.8), kind=kLoop, calls=%fused_computation | loop fusion | bytes 278528 | tf_op jit(solution)/shard_map/squeeze | solution.py:408
  7.8 3.0 %collective-permute-start.15 = (f32[136,128]{1,0:T(8,128)S(1)}, f32[136,128]{1,0:T(8,128)S(1)}, u32[]{:S(2)}, u32[]{:S(2)}) collective-permute-start(f32[136,128]{1,0:T(8,128)S(1)} %get-tuple-element.9), channel_id=1, source_target_pairs={{0,1},{1,0},{2,3},{3,2},{4,5},{5,4},{6,7},{7,6},{8,9},{9,8},{10,11... | collective-permute-start | bytes 208904 | tf_op jit(solution)/shard_map/ppermute | solution.py:408
  10.8 0.0 collective-permute-start.7
  10.8 1.5 %collective-permute-start.3 = (f32[136,128]{1,0:T(8,128)S(1)}, f32[136,128]{1,0:T(8,128)S(1)}, u32[]{:S(2)}, u32[]{:S(2)}) collective-permute-start(f32[136,128]{1,0:T(8,128)S(1)} %get-tuple-element.10.refs_0_), channel_id=1, source_target_pairs={{0,4},{2,6},{4,0},{6,2},{8,12},{10,14},{12,8},{14,10},{16,20},{18,... | collective-permute-start | bytes 208904 | tf_op jit(solution)/shard_map/ppermute | solution.py:406
  12.3 3.6 %collective-permute-start.2 = (f32[136,128]{1,0:T(8,128)S(1)}, f32[136,128]{1,0:T(8,128)S(1)}, u32[]{:S(2)}, u32[]{:S(2)}) collective-permute-start(f32[136,128]{1,0:T(8,128)S(1)} %get-tuple-element.10.refs_0_), channel_id=1, source_target_pairs={{0,24},{2,26},{4,28},{6,30},{8,16},{10,18},{12,20},{14,22},{16,8},... | collective-permute-start | bytes 208904 | tf_op jit(solution)/shard_map/ppermute | solution.py:406
  15.9 0.0 collective-permute-start.1
  15.9 0.0 collective-permute-done.15.refs_16_
  15.9 0.8 %collective-permute-start = (f32[136,128]{1,0:T(8,128)S(1)}, f32[136,128]{1,0:T(8,128)S(1)}, u32[]{:S(2)}, u32[]{:S(2)}) collective-permute-start(f32[136,128]{1,0:T(8,128)S(1)} %get-tuple-element.10.refs_0_), channel_id=1, source_target_pairs={{0,8},{2,10},{4,12},{6,14},{8,0},{10,2},{12,4},{14,6},{16,24},{18,... | collective-permute-start | bytes 208904 | tf_op jit(solution)/shard_map/ppermute | solution.py:406
  16.7 0.0 collective-permute-done.7.refs_8_
  16.7 0.0 collective-permute-start.23
  16.7 0.0 collective-permute-done.3.refs_4_
  16.7 0.6 collective-permute-start.19
  17.3 1.5 %collective-permute-done.2.refs_3_ = f32[136,128]{1,0:T(8,128)S(1)} collective-permute-done((f32[136,128]{1,0:T(8,128)S(1)}, f32[136,128]{1,0:T(8,128)S(1)}, u32[]{:S(2)}, u32[]{:S(2)}) %collective-permute-start.2) | collective-permute-done | bytes 69664 | tf_op jit(solution)/shard_map/ppermute | solution.py:406
  18.8 4.1 %collective-permute-start.18 = (f32[136,128]{1,0:T(8,128)S(1)}, f32[136,128]{1,0:T(8,128)S(1)}, u32[]{:S(2)}, u32[]{:S(2)}) collective-permute-start(f32[136,128]{1,0:T(8,128)S(1)} %collective-permute-done.15.refs_16_), channel_id=1, source_target_pairs={{0,24},{2,26},{4,28},{6,30},{8,16},{10,18},{12,20},{14,22},{16,8},... | collective-permute-start | bytes 208904 | tf_op jit(solution)/shard_map/ppermute | solution.py:406
  22.9 0.1 collective-permute-done.1.refs_2_
  22.9 0.5 collective-permute-start.17
  23.4 0.0 collective-permute-done.refs_1_
  23.4 2.2 %collective-permute-start.16 = (f32[136,128]{1,0:T(8,128)S(1)}, f32[136,128]{1,0:T(8,128)S(1)}, u32[]{:S(2)}, u32[]{:S(2)}) collective-permute-start(f32[136,128]{1,0:T(8,128)S(1)} %collective-permute-done.15.refs_16_), channel_id=1, source_target_pairs={{0,8},{2,10},{4,12},{6,14},{8,0},{10,2},{12,4},{14,6},{16,24},{18,... | collective-permute-start | bytes 208904 | tf_op jit(solution)/shard_map/ppermute | solution.py:406
  25.6 0.0 collective-permute-done.23.refs_24_
  25.7 0.0 collective-permute-start.11
  25.7 0.0 collective-permute-done.19.refs_20_
  25.7 0.5 collective-permute-start.10
  26.2 0.0 collective-permute-done.18.refs_19_
  26.2 0.4 collective-permute-start.6
  26.5 2.4 %collective-permute-done.17.refs_18_ = f32[136,128]{1,0:T(8,128)S(1)} collective-permute-done((f32[136,128]{1,0:T(8,128)S(1)}, f32[136,128]{1,0:T(8,128)S(1)}, u32[]{:S(2)}, u32[]{:S(2)}) %collective-permute-start.17) | collective-permute-done | bytes 69664 | tf_op jit(solution)/shard_map/ppermute | solution.py:406
  28.9 0.0 collective-permute-start.9
  28.9 0.0 collective-permute-done.16.refs_17_
  29.0 0.5 collective-permute-start.5
  29.5 0.0 collective-permute-done.11.refs_12_
  29.5 0.2 collective-permute-start.8
  29.6 0.0 collective-permute-done.10.refs_11_
  29.7 1.5 %collective-permute-start.4 = (f32[136,128]{1,0:T(8,128)S(1)}, f32[136,128]{1,0:T(8,128)S(1)}, u32[]{:S(2)}, u32[]{:S(2)}) collective-permute-start(f32[136,128]{1,0:T(8,128)S(1)} %collective-permute-done.refs_1_), channel_id=1, source_target_pairs={{0,4},{2,6},{4,0},{6,2},{8,12},{10,14},{12,8},{14,10},{16,20},{18,... | collective-permute-start | bytes 208904 | tf_op jit(solution)/shard_map/ppermute | solution.py:406
  31.2 0.0 collective-permute-done.6.refs_7_
  31.2 0.1 collective-permute-start.27
  31.3 0.0 collective-permute-done.9.refs_10_
  31.3 0.4 collective-permute-start.26
  31.7 2.3 %collective-permute-done.5.refs_6_ = f32[136,128]{1,0:T(8,128)S(1)} collective-permute-done((f32[136,128]{1,0:T(8,128)S(1)}, f32[136,128]{1,0:T(8,128)S(1)}, u32[]{:S(2)}, u32[]{:S(2)}) %collective-permute-start.5) | collective-permute-done | bytes 69664 | tf_op jit(solution)/shard_map/ppermute | solution.py:406
  34.0 0.0 collective-permute-start.22
  34.1 0.0 collective-permute-done.8.refs_9_
  34.1 0.1 collective-permute-start.25
  34.1 0.9 %collective-permute-done.4.refs_5_ = f32[136,128]{1,0:T(8,128)S(1)} collective-permute-done((f32[136,128]{1,0:T(8,128)S(1)}, f32[136,128]{1,0:T(8,128)S(1)}, u32[]{:S(2)}, u32[]{:S(2)}) %collective-permute-start.4) | collective-permute-done | bytes 69664 | tf_op jit(solution)/shard_map/ppermute | solution.py:406
  35.0 1.2 %collective-permute-start.21 = (f32[136,128]{1,0:T(8,128)S(1)}, f32[136,128]{1,0:T(8,128)S(1)}, u32[]{:S(2)}, u32[]{:S(2)}) collective-permute-start(f32[136,128]{1,0:T(8,128)S(1)} %collective-permute-done.17.refs_18_), channel_id=1, source_target_pairs={{0,4},{2,6},{4,0},{6,2},{8,12},{10,14},{12,8},{14,10},{16,20},{18,... | collective-permute-start | bytes 208904 | tf_op jit(solution)/shard_map/ppermute | solution.py:406
  36.2 0.0 collective-permute-done.27.refs_28_
  36.2 0.1 collective-permute-start.24
  36.3 0.0 collective-permute-done.26.refs_27_
  36.3 0.8 %collective-permute-start.20 = (f32[136,128]{1,0:T(8,128)S(1)}, f32[136,128]{1,0:T(8,128)S(1)}, u32[]{:S(2)}, u32[]{:S(2)}) collective-permute-start(f32[136,128]{1,0:T(8,128)S(1)} %collective-permute-done.16.refs_17_), channel_id=1, source_target_pairs={{0,4},{2,6},{4,0},{6,2},{8,12},{10,14},{12,8},{14,10},{16,20},{18,... | collective-permute-start | bytes 208904 | tf_op jit(solution)/shard_map/ppermute | solution.py:406
  37.1 1.8 %collective-permute-done.22.refs_23_ = f32[136,128]{1,0:T(8,128)S(1)} collective-permute-done((f32[136,128]{1,0:T(8,128)S(1)}, f32[136,128]{1,0:T(8,128)S(1)}, u32[]{:S(2)}, u32[]{:S(2)}) %collective-permute-start.22) | collective-permute-done | bytes 69664 | tf_op jit(solution)/shard_map/ppermute | solution.py:406
  38.9 0.0 collective-permute-start.14
  38.9 0.0 collective-permute-done.25.refs_26_
  39.0 0.5 collective-permute-start.13
  39.5 0.6 %collective-permute-done.21.refs_22_ = f32[136,128]{1,0:T(8,128)S(1)} collective-permute-done((f32[136,128]{1,0:T(8,128)S(1)}, f32[136,128]{1,0:T(8,128)S(1)}, u32[]{:S(2)}, u32[]{:S(2)}) %collective-permute-start.21) | collective-permute-done | bytes 69664 | tf_op jit(solution)/shard_map/ppermute | solution.py:406
  40.1 0.0 collective-permute-start.12
  40.1 0.5 collective-permute-start.30
  40.6 0.6 collective-permute-done.20.refs_21_
  41.2 0.0 collective-permute-start.29
  41.2 0.5 collective-permute-start.28
  41.7 0.0 collective-permute-done.13.refs_14_
  41.7 0.0 collective-permute-done.12.refs_13_
  41.7 0.7 %collective-permute-done.29.refs_30_ = f32[136,128]{1,0:T(8,128)S(1)} collective-permute-done((f32[136,128]{1,0:T(8,128)S(1)}, f32[136,128]{1,0:T(8,128)S(1)}, u32[]{:S(2)}, u32[]{:S(2)}) %collective-permute-start.29) | collective-permute-done | bytes 69664 | tf_op jit(solution)/shard_map/ppermute | solution.py:406
  42.4 0.2 collective-permute-done.28.refs_29_
  42.9 0.2 copy-done.30
  43.1 0.2 copy-done.31
  43.2 15.8 %shard_map.131 = f32[16384,128]{1,0:T(8,128)} custom-call(s32[1]{0:T(128)} %bitcast.7.start_ref, f32[136,128]{1,0:T(8,128)} %copy-done, f32[136,128]{1,0:T(8,128)} %copy-done.6, f32[136,128]{1,0:T(8,128)} %copy-done.5, f32[136,128]{1,0:T(8,128)} %copy-done.4, f32[136,128]{1,0:T(8,128)} %copy-done.3, f32[136,128]{1,0:T(8,128)} %copy-done.18, ...), custom_call_target="tpu_custom_call" | custom-call | tf_op jit(solution)/shard_map/pallas_call | solution.py:476
  (65 shorter events, 0.1 us)
Async XLA Ops:
  7.8 34.9 %copy-start = (f32[136,128]{1,0:T(8,128)}, f32[136,128]{1,0:T(8,128)S(1)}, u32[]{:S(2)}) copy-start(f32[136,128]{1,0:T(8,128)S(1)} %get-tuple-element.10.refs_0_) | copy-start | bytes 208900
  7.8 8.2 %collective-permute-start.15 = (f32[136,128]{1,0:T(8,128)S(1)}, f32[136,128]{1,0:T(8,128)S(1)}, u32[]{:S(2)}, u32[]{:S(2)}) collective-permute-start(f32[136,128]{1,0:T(8,128)S(1)} %get-tuple-element.9), channel_id=1, source_target_pairs={{0,1},{1,0},{2,3},{3,2},{4,5},{5,4},{6,7},{7,6},{8,9},{9,8},{10,11... | collective-permute-start | bytes 208904 | tf_op jit(solution)/shard_map/ppermute | solution.py:408
  10.8 5.9 %collective-permute-start.7 = (f32[136,128]{1,0:T(8,128)S(1)}, f32[136,128]{1,0:T(8,128)S(1)}, u32[]{:S(2)}, u32[]{:S(2)}) collective-permute-start(f32[136,128]{1,0:T(8,128)S(1)} %get-tuple-element.10.refs_0_), channel_id=1, source_target_pairs={{0,2},{2,0},{4,6},{6,4},{8,10},{10,8},{12,14},{14,12},{16,18},{18,... | collective-permute-start | bytes 208904 | tf_op jit(solution)/shard_map/ppermute | solution.py:406
  10.8 5.9 %collective-permute-start.3 = (f32[136,128]{1,0:T(8,128)S(1)}, f32[136,128]{1,0:T(8,128)S(1)}, u32[]{:S(2)}, u32[]{:S(2)}) collective-permute-start(f32[136,128]{1,0:T(8,128)S(1)} %get-tuple-element.10.refs_0_), channel_id=1, source_target_pairs={{0,4},{2,6},{4,0},{6,2},{8,12},{10,14},{12,8},{14,10},{16,20},{18,... | collective-permute-start | bytes 208904 | tf_op jit(solution)/shard_map/ppermute | solution.py:406
  12.3 6.5 %collective-permute-start.2 = (f32[136,128]{1,0:T(8,128)S(1)}, f32[136,128]{1,0:T(8,128)S(1)}, u32[]{:S(2)}, u32[]{:S(2)}) collective-permute-start(f32[136,128]{1,0:T(8,128)S(1)} %get-tuple-element.10.refs_0_), channel_id=1, source_target_pairs={{0,24},{2,26},{4,28},{6,30},{8,16},{10,18},{12,20},{14,22},{16,8},... | collective-permute-start | bytes 208904 | tf_op jit(solution)/shard_map/ppermute | solution.py:406
  15.9 7.0 %collective-permute-start.1 = (f32[136,128]{1,0:T(8,128)S(1)}, f32[136,128]{1,0:T(8,128)S(1)}, u32[]{:S(2)}, u32[]{:S(2)}) collective-permute-start(f32[136,128]{1,0:T(8,128)S(1)} %get-tuple-element.10.refs_0_), channel_id=1, source_target_pairs={{0,16},{2,18},{4,20},{6,22},{8,24},{10,26},{12,28},{14,30},{16,0},... | collective-permute-start | bytes 208904 | tf_op jit(solution)/shard_map/ppermute | solution.py:406
  15.9 26.7 %copy-start.1 = (f32[136,128]{1,0:T(8,128)}, f32[136,128]{1,0:T(8,128)S(1)}, u32[]{:S(2)}) copy-start(f32[136,128]{1,0:T(8,128)S(1)} %collective-permute-done.15.refs_16_) | copy-start | bytes 208900
  15.9 7.5 %collective-permute-start = (f32[136,128]{1,0:T(8,128)S(1)}, f32[136,128]{1,0:T(8,128)S(1)}, u32[]{:S(2)}, u32[]{:S(2)}) collective-permute-start(f32[136,128]{1,0:T(8,128)S(1)} %get-tuple-element.10.refs_0_), channel_id=1, source_target_pairs={{0,8},{2,10},{4,12},{6,14},{8,0},{10,2},{12,4},{14,6},{16,24},{18,... | collective-permute-start | bytes 208904 | tf_op jit(solution)/shard_map/ppermute | solution.py:406
  16.7 25.9 %copy-start.2 = (f32[136,128]{1,0:T(8,128)}, f32[136,128]{1,0:T(8,128)S(1)}, u32[]{:S(2)}) copy-start(f32[136,128]{1,0:T(8,128)S(1)} %collective-permute-done.7.refs_8_) | copy-start | bytes 208900
  16.7 8.9 %collective-permute-start.23 = (f32[136,128]{1,0:T(8,128)S(1)}, f32[136,128]{1,0:T(8,128)S(1)}, u32[]{:S(2)}, u32[]{:S(2)}) collective-permute-start(f32[136,128]{1,0:T(8,128)S(1)} %collective-permute-done.15.refs_16_), channel_id=1, source_target_pairs={{0,2},{2,0},{4,6},{6,4},{8,10},{10,8},{12,14},{14,12},{16,18},{18,... | collective-permute-start | bytes 208904 | tf_op jit(solution)/shard_map/ppermute | solution.py:406
  16.7 25.9 %copy-start.3 = (f32[136,128]{1,0:T(8,128)}, f32[136,128]{1,0:T(8,128)S(1)}, u32[]{:S(2)}) copy-start(f32[136,128]{1,0:T(8,128)S(1)} %collective-permute-done.3.refs_4_) | copy-start | bytes 208900
  16.7 8.9 %collective-permute-start.19 = (f32[136,128]{1,0:T(8,128)S(1)}, f32[136,128]{1,0:T(8,128)S(1)}, u32[]{:S(2)}, u32[]{:S(2)}) collective-permute-start(f32[136,128]{1,0:T(8,128)S(1)} %collective-permute-done.15.refs_16_), channel_id=1, source_target_pairs={{0,4},{2,6},{4,0},{6,2},{8,12},{10,14},{12,8},{14,10},{16,20},{18,... | collective-permute-start | bytes 208904 | tf_op jit(solution)/shard_map/ppermute | solution.py:406
  18.8 23.8 %copy-start.4 = (f32[136,128]{1,0:T(8,128)}, f32[136,128]{1,0:T(8,128)S(1)}, u32[]{:S(2)}) copy-start(f32[136,128]{1,0:T(8,128)S(1)} %collective-permute-done.2.refs_3_) | copy-start | bytes 208900
  18.8 7.4 %collective-permute-start.18 = (f32[136,128]{1,0:T(8,128)S(1)}, f32[136,128]{1,0:T(8,128)S(1)}, u32[]{:S(2)}, u32[]{:S(2)}) collective-permute-start(f32[136,128]{1,0:T(8,128)S(1)} %collective-permute-done.15.refs_16_), channel_id=1, source_target_pairs={{0,24},{2,26},{4,28},{6,30},{8,16},{10,18},{12,20},{14,22},{16,8},... | collective-permute-start | bytes 208904 | tf_op jit(solution)/shard_map/ppermute | solution.py:406
  22.9 19.7 %copy-start.5 = (f32[136,128]{1,0:T(8,128)}, f32[136,128]{1,0:T(8,128)S(1)}, u32[]{:S(2)}) copy-start(f32[136,128]{1,0:T(8,128)S(1)} %collective-permute-done.1.refs_2_) | copy-start | bytes 208900
  22.9 6.0 %collective-permute-start.17 = (f32[136,128]{1,0:T(8,128)S(1)}, f32[136,128]{1,0:T(8,128)S(1)}, u32[]{:S(2)}, u32[]{:S(2)}) collective-permute-start(f32[136,128]{1,0:T(8,128)S(1)} %collective-permute-done.15.refs_16_), channel_id=1, source_target_pairs={{0,16},{2,18},{4,20},{6,22},{8,24},{10,26},{12,28},{14,30},{16,0},... | collective-permute-start | bytes 208904 | tf_op jit(solution)/shard_map/ppermute | solution.py:406
  23.4 19.2 %copy-start.6 = (f32[136,128]{1,0:T(8,128)}, f32[136,128]{1,0:T(8,128)S(1)}, u32[]{:S(2)}) copy-start(f32[136,128]{1,0:T(8,128)S(1)} %collective-permute-done.refs_1_) | copy-start | bytes 208900
  23.4 5.5 %collective-permute-start.16 = (f32[136,128]{1,0:T(8,128)S(1)}, f32[136,128]{1,0:T(8,128)S(1)}, u32[]{:S(2)}, u32[]{:S(2)}) collective-permute-start(f32[136,128]{1,0:T(8,128)S(1)} %collective-permute-done.15.refs_16_), channel_id=1, source_target_pairs={{0,8},{2,10},{4,12},{6,14},{8,0},{10,2},{12,4},{14,6},{16,24},{18,... | collective-permute-start | bytes 208904 | tf_op jit(solution)/shard_map/ppermute | solution.py:406
  25.6 17.0 %copy-start.7 = (f32[136,128]{1,0:T(8,128)}, f32[136,128]{1,0:T(8,128)S(1)}, u32[]{:S(2)}) copy-start(f32[136,128]{1,0:T(8,128)S(1)} %collective-permute-done.23.refs_24_) | copy-start | bytes 208900
  25.7 3.8 %collective-permute-start.11 = (f32[136,128]{1,0:T(8,128)S(1)}, f32[136,128]{1,0:T(8,128)S(1)}, u32[]{:S(2)}, u32[]{:S(2)}) collective-permute-start(f32[136,128]{1,0:T(8,128)S(1)} %collective-permute-done.3.refs_4_), channel_id=1, source_target_pairs={{0,2},{2,0},{4,6},{6,4},{8,10},{10,8},{12,14},{14,12},{16,18},{18,... | collective-permute-start | bytes 208904 | tf_op jit(solution)/shard_map/ppermute | solution.py:406
  25.7 17.0 %copy-start.8 = (f32[136,128]{1,0:T(8,128)}, f32[136,128]{1,0:T(8,128)S(1)}, u32[]{:S(2)}) copy-start(f32[136,128]{1,0:T(8,128)S(1)} %collective-permute-done.19.refs_20_) | copy-start | bytes 208900
  25.7 4.0 %collective-permute-start.10 = (f32[136,128]{1,0:T(8,128)S(1)}, f32[136,128]{1,0:T(8,128)S(1)}, u32[]{:S(2)}, u32[]{:S(2)}) collective-permute-start(f32[136,128]{1,0:T(8,128)S(1)} %collective-permute-done.2.refs_3_), channel_id=1, source_target_pairs={{0,2},{2,0},{4,6},{6,4},{8,10},{10,8},{12,14},{14,12},{16,18},{18,... | collective-permute-start | bytes 208904 | tf_op jit(solution)/shard_map/ppermute | solution.py:406
  26.2 16.5 %copy-start.9 = (f32[136,128]{1,0:T(8,128)}, f32[136,128]{1,0:T(8,128)S(1)}, u32[]{:S(2)}) copy-start(f32[136,128]{1,0:T(8,128)S(1)} %collective-permute-done.18.refs_19_) | copy-start | bytes 208900
  26.2 5.0 %collective-permute-start.6 = (f32[136,128]{1,0:T(8,128)S(1)}, f32[136,128]{1,0:T(8,128)S(1)}, u32[]{:S(2)}, u32[]{:S(2)}) collective-permute-start(f32[136,128]{1,0:T(8,128)S(1)} %collective-permute-done.2.refs_3_), channel_id=1, source_target_pairs={{0,4},{2,6},{4,0},{6,2},{8,12},{10,14},{12,8},{14,10},{16,20},{18,... | collective-permute-start | bytes 208904 | tf_op jit(solution)/shard_map/ppermute | solution.py:406
  28.9 13.8 %copy-start.10 = (f32[136,128]{1,0:T(8,128)}, f32[136,128]{1,0:T(8,128)S(1)}, u32[]{:S(2)}) copy-start(f32[136,128]{1,0:T(8,128)S(1)} %collective-permute-done.17.refs_18_) | copy-start | bytes 208900
  28.9 2.4 %collective-permute-start.9 = (f32[136,128]{1,0:T(8,128)S(1)}, f32[136,128]{1,0:T(8,128)S(1)}, u32[]{:S(2)}, u32[]{:S(2)}) collective-permute-start(f32[136,128]{1,0:T(8,128)S(1)} %collective-permute-done.1.refs_2_), channel_id=1, source_target_pairs={{0,2},{2,0},{4,6},{6,4},{8,10},{10,8},{12,14},{14,12},{16,18},{18,... | collective-permute-start | bytes 208904 | tf_op jit(solution)/shard_map/ppermute | solution.py:406
  29.0 13.7 %copy-start.11 = (f32[136,128]{1,0:T(8,128)}, f32[136,128]{1,0:T(8,128)S(1)}, u32[]{:S(2)}) copy-start(f32[136,128]{1,0:T(8,128)S(1)} %collective-permute-done.16.refs_17_) | copy-start | bytes 208900
  29.0 5.1 %collective-permute-start.5 = (f32[136,128]{1,0:T(8,128)S(1)}, f32[136,128]{1,0:T(8,128)S(1)}, u32[]{:S(2)}, u32[]{:S(2)}) collective-permute-start(f32[136,128]{1,0:T(8,128)S(1)} %collective-permute-done.1.refs_2_), channel_id=1, source_target_pairs={{0,4},{2,6},{4,0},{6,2},{8,12},{10,14},{12,8},{14,10},{16,20},{18,... | collective-permute-start | bytes 208904 | tf_op jit(solution)/shard_map/ppermute | solution.py:406
  29.5 13.2 %copy-start.12 = (f32[136,128]{1,0:T(8,128)}, f32[136,128]{1,0:T(8,128)S(1)}, u32[]{:S(2)}) copy-start(f32[136,128]{1,0:T(8,128)S(1)} %collective-permute-done.11.refs_12_) | copy-start | bytes 208900
  29.5 4.6 %collective-permute-start.8 = (f32[136,128]{1,0:T(8,128)S(1)}, f32[136,128]{1,0:T(8,128)S(1)}, u32[]{:S(2)}, u32[]{:S(2)}) collective-permute-start(f32[136,128]{1,0:T(8,128)S(1)} %collective-permute-done.refs_1_), channel_id=1, source_target_pairs={{0,2},{2,0},{4,6},{6,4},{8,10},{10,8},{12,14},{14,12},{16,18},{18,... | collective-permute-start | bytes 208904 | tf_op jit(solution)/shard_map/ppermute | solution.py:406
  29.7 13.1 %copy-start.13 = (f32[136,128]{1,0:T(8,128)}, f32[136,128]{1,0:T(8,128)S(1)}, u32[]{:S(2)}) copy-start(f32[136,128]{1,0:T(8,128)S(1)} %collective-permute-done.10.refs_11_) | copy-start | bytes 208900
  29.7 5.3 %collective-permute-start.4 = (f32[136,128]{1,0:T(8,128)S(1)}, f32[136,128]{1,0:T(8,128)S(1)}, u32[]{:S(2)}, u32[]{:S(2)}) collective-permute-start(f32[136,128]{1,0:T(8,128)S(1)} %collective-permute-done.refs_1_), channel_id=1, source_target_pairs={{0,4},{2,6},{4,0},{6,2},{8,12},{10,14},{12,8},{14,10},{16,20},{18,... | collective-permute-start | bytes 208904 | tf_op jit(solution)/shard_map/ppermute | solution.py:406
  31.2 11.5 %copy-start.14 = (f32[136,128]{1,0:T(8,128)}, f32[136,128]{1,0:T(8,128)S(1)}, u32[]{:S(2)}) copy-start(f32[136,128]{1,0:T(8,128)S(1)} %collective-permute-done.6.refs_7_) | copy-start | bytes 208900
  31.2 5.0 %collective-permute-start.27 = (f32[136,128]{1,0:T(8,128)S(1)}, f32[136,128]{1,0:T(8,128)S(1)}, u32[]{:S(2)}, u32[]{:S(2)}) collective-permute-start(f32[136,128]{1,0:T(8,128)S(1)} %collective-permute-done.19.refs_20_), channel_id=1, source_target_pairs={{0,2},{2,0},{4,6},{6,4},{8,10},{10,8},{12,14},{14,12},{16,18},{18,... | collective-permute-start | bytes 208904 | tf_op jit(solution)/shard_map/ppermute | solution.py:406
  31.3 11.5 %copy-start.15 = (f32[136,128]{1,0:T(8,128)}, f32[136,128]{1,0:T(8,128)S(1)}, u32[]{:S(2)}) copy-start(f32[136,128]{1,0:T(8,128)S(1)} %collective-permute-done.9.refs_10_) | copy-start | bytes 208900
  31.3 5.1 %collective-permute-start.26 = (f32[136,128]{1,0:T(8,128)S(1)}, f32[136,128]{1,0:T(8,128)S(1)}, u32[]{:S(2)}, u32[]{:S(2)}) collective-permute-start(f32[136,128]{1,0:T(8,128)S(1)} %collective-permute-done.18.refs_19_), channel_id=1, source_target_pairs={{0,2},{2,0},{4,6},{6,4},{8,10},{10,8},{12,14},{14,12},{16,18},{18,... | collective-permute-start | bytes 208904 | tf_op jit(solution)/shard_map/ppermute | solution.py:406
  34.0 8.7 %copy-start.16 = (f32[136,128]{1,0:T(8,128)}, f32[136,128]{1,0:T(8,128)S(1)}, u32[]{:S(2)}) copy-start(f32[136,128]{1,0:T(8,128)S(1)} %collective-permute-done.5.refs_6_) | copy-start | bytes 208900
  34.0 4.9 %collective-permute-start.22 = (f32[136,128]{1,0:T(8,128)S(1)}, f32[136,128]{1,0:T(8,128)S(1)}, u32[]{:S(2)}, u32[]{:S(2)}) collective-permute-start(f32[136,128]{1,0:T(8,128)S(1)} %collective-permute-done.18.refs_19_), channel_id=1, source_target_pairs={{0,4},{2,6},{4,0},{6,2},{8,12},{10,14},{12,8},{14,10},{16,20},{18,... | collective-permute-start | bytes 208904 | tf_op jit(solution)/shard_map/ppermute | solution.py:406
  34.1 8.7 %copy-start.17 = (f32[136,128]{1,0:T(8,128)}, f32[136,128]{1,0:T(8,128)S(1)}, u32[]{:S(2)}) copy-start(f32[136,128]{1,0:T(8,128)S(1)} %collective-permute-done.8.refs_9_) | copy-start | bytes 208900
  34.1 4.9 %collective-permute-start.25 = (f32[136,128]{1,0:T(8,128)S(1)}, f32[136,128]{1,0:T(8,128)S(1)}, u32[]{:S(2)}, u32[]{:S(2)}) collective-permute-start(f32[136,128]{1,0:T(8,128)S(1)} %collective-permute-done.17.refs_18_), channel_id=1, source_target_pairs={{0,2},{2,0},{4,6},{6,4},{8,10},{10,8},{12,14},{14,12},{16,18},{18,... | collective-permute-start | bytes 208904 | tf_op jit(solution)/shard_map/ppermute | solution.py:406
  35.0 7.8 %copy-start.18 = (f32[136,128]{1,0:T(8,128)}, f32[136,128]{1,0:T(8,128)S(1)}, u32[]{:S(2)}) copy-start(f32[136,128]{1,0:T(8,128)S(1)} %collective-permute-done.4.refs_5_) | copy-start | bytes 208900
  35.0 5.1 %collective-permute-start.21 = (f32[136,128]{1,0:T(8,128)S(1)}, f32[136,128]{1,0:T(8,128)S(1)}, u32[]{:S(2)}, u32[]{:S(2)}) collective-permute-start(f32[136,128]{1,0:T(8,128)S(1)} %collective-permute-done.17.refs_18_), channel_id=1, source_target_pairs={{0,4},{2,6},{4,0},{6,2},{8,12},{10,14},{12,8},{14,10},{16,20},{18,... | collective-permute-start | bytes 208904 | tf_op jit(solution)/shard_map/ppermute | solution.py:406
  36.2 6.6 %copy-start.19 = (f32[136,128]{1,0:T(8,128)}, f32[136,128]{1,0:T(8,128)S(1)}, u32[]{:S(2)}) copy-start(f32[136,128]{1,0:T(8,128)S(1)} %collective-permute-done.27.refs_28_) | copy-start | bytes 208900
  36.2 3.9 %collective-permute-start.24 = (f32[136,128]{1,0:T(8,128)S(1)}, f32[136,128]{1,0:T(8,128)S(1)}, u32[]{:S(2)}, u32[]{:S(2)}) collective-permute-start(f32[136,128]{1,0:T(8,128)S(1)} %collective-permute-done.16.refs_17_), channel_id=1, source_target_pairs={{0,2},{2,0},{4,6},{6,4},{8,10},{10,8},{12,14},{14,12},{16,18},{18,... | collective-permute-start | bytes 208904 | tf_op jit(solution)/shard_map/ppermute | solution.py:406
  36.3 6.5 %copy-start.20 = (f32[136,128]{1,0:T(8,128)}, f32[136,128]{1,0:T(8,128)S(1)}, u32[]{:S(2)}) copy-start(f32[136,128]{1,0:T(8,128)S(1)} %collective-permute-done.26.refs_27_) | copy-start | bytes 208900
  36.3 4.8 %collective-permute-start.20 = (f32[136,128]{1,0:T(8,128)S(1)}, f32[136,128]{1,0:T(8,128)S(1)}, u32[]{:S(2)}, u32[]{:S(2)}) collective-permute-start(f32[136,128]{1,0:T(8,128)S(1)} %collective-permute-done.16.refs_17_), channel_id=1, source_target_pairs={{0,4},{2,6},{4,0},{6,2},{8,12},{10,14},{12,8},{14,10},{16,20},{18,... | collective-permute-start | bytes 208904 | tf_op jit(solution)/shard_map/ppermute | solution.py:406
  38.9 3.9 %copy-start.21 = (f32[136,128]{1,0:T(8,128)}, f32[136,128]{1,0:T(8,128)S(1)}, u32[]{:S(2)}) copy-start(f32[136,128]{1,0:T(8,128)S(1)} %collective-permute-done.22.refs_23_) | copy-start | bytes 208900
  38.9 2.2 %collective-permute-start.14 = (f32[136,128]{1,0:T(8,128)S(1)}, f32[136,128]{1,0:T(8,128)S(1)}, u32[]{:S(2)}, u32[]{:S(2)}) collective-permute-start(f32[136,128]{1,0:T(8,128)S(1)} %collective-permute-done.6.refs_7_), channel_id=1, source_target_pairs={{0,2},{2,0},{4,6},{6,4},{8,10},{10,8},{12,14},{14,12},{16,18},{18,... | collective-permute-start | bytes 208904 | tf_op jit(solution)/shard_map/ppermute | solution.py:406
  39.0 3.9 %copy-start.22 = (f32[136,128]{1,0:T(8,128)}, f32[136,128]{1,0:T(8,128)S(1)}, u32[]{:S(2)}) copy-start(f32[136,128]{1,0:T(8,128)S(1)} %collective-permute-done.25.refs_26_) | copy-start | bytes 208900
  39.0 2.7 %collective-permute-start.13 = (f32[136,128]{1,0:T(8,128)S(1)}, f32[136,128]{1,0:T(8,128)S(1)}, u32[]{:S(2)}, u32[]{:S(2)}) collective-permute-start(f32[136,128]{1,0:T(8,128)S(1)} %collective-permute-done.5.refs_6_), channel_id=1, source_target_pairs={{0,2},{2,0},{4,6},{6,4},{8,10},{10,8},{12,14},{14,12},{16,18},{18,... | collective-permute-start | bytes 208904 | tf_op jit(solution)/shard_map/ppermute | solution.py:406
  40.1 2.7 %copy-start.23 = (f32[136,128]{1,0:T(8,128)}, f32[136,128]{1,0:T(8,128)S(1)}, u32[]{:S(2)}) copy-start(f32[136,128]{1,0:T(8,128)S(1)} %collective-permute-done.21.refs_22_) | copy-start | bytes 208900
  40.1 1.6 %collective-permute-start.12 = (f32[136,128]{1,0:T(8,128)S(1)}, f32[136,128]{1,0:T(8,128)S(1)}, u32[]{:S(2)}, u32[]{:S(2)}) collective-permute-start(f32[136,128]{1,0:T(8,128)S(1)} %collective-permute-done.4.refs_5_), channel_id=1, source_target_pairs={{0,2},{2,0},{4,6},{6,4},{8,10},{10,8},{12,14},{14,12},{16,18},{18,... | collective-permute-start | bytes 208904 | tf_op jit(solution)/shard_map/ppermute | solution.py:406
  40.1 2.7 %copy-start.24 = (f32[136,128]{1,0:T(8,128)}, f32[136,128]{1,0:T(8,128)S(1)}, u32[]{:S(2)}) copy-start(f32[136,128]{1,0:T(8,128)S(1)} %collective-permute-done.24.refs_25_) | copy-start | bytes 208900
  40.1 1.6 %collective-permute-start.30 = (f32[136,128]{1,0:T(8,128)S(1)}, f32[136,128]{1,0:T(8,128)S(1)}, u32[]{:S(2)}, u32[]{:S(2)}) collective-permute-start(f32[136,128]{1,0:T(8,128)S(1)} %collective-permute-done.22.refs_23_), channel_id=1, source_target_pairs={{0,2},{2,0},{4,6},{6,4},{8,10},{10,8},{12,14},{14,12},{16,18},{18,... | collective-permute-start | bytes 208904 | tf_op jit(solution)/shard_map/ppermute | solution.py:406
  41.2 1.7 %copy-start.25 = (f32[136,128]{1,0:T(8,128)}, f32[136,128]{1,0:T(8,128)S(1)}, u32[]{:S(2)}) copy-start(f32[136,128]{1,0:T(8,128)S(1)} %collective-permute-done.20.refs_21_) | copy-start | bytes 208900
  41.2 1.3 %collective-permute-start.29 = (f32[136,128]{1,0:T(8,128)S(1)}, f32[136,128]{1,0:T(8,128)S(1)}, u32[]{:S(2)}, u32[]{:S(2)}) collective-permute-start(f32[136,128]{1,0:T(8,128)S(1)} %collective-permute-done.21.refs_22_), channel_id=1, source_target_pairs={{0,2},{2,0},{4,6},{6,4},{8,10},{10,8},{12,14},{14,12},{16,18},{18,... | collective-permute-start | bytes 208904 | tf_op jit(solution)/shard_map/ppermute | solution.py:406
  41.2 1.7 %copy-start.26 = (f32[136,128]{1,0:T(8,128)}, f32[136,128]{1,0:T(8,128)S(1)}, u32[]{:S(2)}) copy-start(f32[136,128]{1,0:T(8,128)S(1)} %collective-permute-done.14.refs_15_) | copy-start | bytes 208900
  41.2 1.4 %collective-permute-start.28 = (f32[136,128]{1,0:T(8,128)S(1)}, f32[136,128]{1,0:T(8,128)S(1)}, u32[]{:S(2)}, u32[]{:S(2)}) collective-permute-start(f32[136,128]{1,0:T(8,128)S(1)} %collective-permute-done.20.refs_21_), channel_id=1, source_target_pairs={{0,2},{2,0},{4,6},{6,4},{8,10},{10,8},{12,14},{14,12},{16,18},{18,... | collective-permute-start | bytes 208904 | tf_op jit(solution)/shard_map/ppermute | solution.py:406
  41.7 1.2 %copy-start.27 = (f32[136,128]{1,0:T(8,128)}, f32[136,128]{1,0:T(8,128)S(1)}, u32[]{:S(2)}) copy-start(f32[136,128]{1,0:T(8,128)S(1)} %collective-permute-done.13.refs_14_) | copy-start | bytes 208900
  41.7 1.2 %copy-start.28 = (f32[136,128]{1,0:T(8,128)}, f32[136,128]{1,0:T(8,128)S(1)}, u32[]{:S(2)}) copy-start(f32[136,128]{1,0:T(8,128)S(1)} %collective-permute-done.12.refs_13_) | copy-start | bytes 208900
  41.7 1.2 %copy-start.29 = (f32[136,128]{1,0:T(8,128)}, f32[136,128]{1,0:T(8,128)S(1)}, u32[]{:S(2)}) copy-start(f32[136,128]{1,0:T(8,128)S(1)} %collective-permute-done.30.refs_31_) | copy-start | bytes 208900
  42.4 0.6 %copy-start.30 = (f32[136,128]{1,0:T(8,128)}, f32[136,128]{1,0:T(8,128)S(1)}, u32[]{:S(2)}) copy-start(f32[136,128]{1,0:T(8,128)S(1)} %collective-permute-done.29.refs_30_) | copy-start | bytes 208900
  42.6 0.6 %copy-start.31 = (f32[136,128]{1,0:T(8,128)}, f32[136,128]{1,0:T(8,128)S(1)}, u32[]{:S(2)}) copy-start(f32[136,128]{1,0:T(8,128)S(1)} %collective-permute-done.28.refs_29_) | copy-start | bytes 208900
